TPU v7x, 32 devices: a whole 2x2x4 slice. The times are simulated.
32 devices in a mesh: fsdp: 4 (over x, core), ctx: 2 (over y), tp: 4 (over z).
Axes of the slice: x: 2, y: 2, z: 4, core: 2. Of those that a mesh axis runs over, the one named last changes fastest.
Arguments:
- tokens: bfloat16 [8, 1024, 768], P('fsdp', 'ctx'), may hold values from -6 to 6
- segments: int32 [8, 1024], P('fsdp', 'ctx'), may hold values from 0 to 3, never falling along the last dimension, each value on 1 to 768 neighbouring positions
- ln_gains: bfloat16 [2, 768], P(None, 'fsdp'), may hold values from 0.5 to 1.5
- ln_biases: bfloat16 [2, 768], P(None, 'fsdp'), may hold values from -1.75 to 1.75
- w_qkv: bfloat16 [3, 768, 768], P(None, 'fsdp', 'tp'), may hold values from -0.21875 to 0.21875
- bias_qv: bfloat16 [2, 12, 64], P(None, 'tp', 'fsdp'), may hold values from -3 to 3
- w_out: bfloat16 [768, 768], P('tp', 'fsdp'), may hold values from -1.25 to 1.25
- out_biases: bfloat16 [2, 768], P(None, 'fsdp'), may hold values from -1.75 to 1.75
- w_up: bfloat16 [768, 3072], P('fsdp', 'tp'), may hold values from -0.21875 to 0.21875
- up_bias: bfloat16 [48, 64], P('tp', 'fsdp'), may hold values from -3 to 3
- w_down: bfloat16 [3072, 768], P('tp', 'fsdp'), may hold values from -0.109375 to 0.109375
- cotangent: bfloat16 [8, 1024, 768], P('fsdp', 'ctx'), may hold values from -6 to 6
Outputs:
- output: bfloat16 [8, 1024, 768], P('fsdp', 'ctx')
- grad_tokens: float32 [8, 1024, 768], P('fsdp', 'ctx')
- grad_ln_gains: float32 [2, 768], P(None, 'fsdp')
- grad_ln_biases: float32 [2, 768], P(None, 'fsdp')
- grad_qkv: float32 [3, 768, 768], P(None, 'fsdp', 'tp')
- grad_bias_qv: float32 [2, 12, 64], P(None, 'tp', 'fsdp')
- grad_out_proj: float32 [768, 768], P('tp', 'fsdp')
- grad_out_biases: float32 [2, 768], P(None, 'fsdp')
- grad_up: float32 [768, 3072], P('fsdp', 'tp')
- grad_up_bias: float32 [48, 64], P('tp', 'fsdp')
- grad_down: float32 [3072, 768], P('tp', 'fsdp')
Inputs may be any that keep to these rules, and one draw needn't show every extreme that they name: `segments`: within each sequence the numbers never fall; each document holds 1 to 768 positions, and one document of each sequence exactly that many.
All inputs are finite; a program needn't handle non-finite values.
Results may differ from a plain program's by a relative error of at most 0.017.
Values may be sent and summed in bfloat16 or wider, within the bound.
No kernel may reach another device: no remote copies, remote signals or barrier semaphores. Data moves between devices by JAX's collectives and lax.ppermute only.
A program may use at most 384 MiB of HBM per device.

v0:
```python
import jax
import jax.numpy as jnp
from jax import lax
from jax.sharding import PartitionSpec as P

HD = 64
eps = 1e-05
masked_score = -1e30


def layer_norm(values_in, gain, shift):
    average = jnp.mean(values_in, axis=-1, keepdims=True)
    centered = values_in - average
    variance = jnp.mean(centered * centered, axis=-1, keepdims=True)
    return centered * lax.rsqrt(variance + eps) * gain + shift


def gelu_tanh(values_in):
    return jax.nn.gelu(values_in, approximate=True)


def block_scores(queries, key_rows, query_place, query_doc, key_place, key_doc):
    scores = (
        jnp.einsum("qhd,khd->hqk", queries, key_rows, preferred_element_type=jnp.float32) * 0.125
    )
    allowed = (query_doc[:, None] == key_doc[None, :]) & (
        key_place[None, :] <= query_place[:, None]
    )
    return jnp.where(allowed[None], scores, masked_score)


def tp_total(make, row_count):
    return lax.psum(make(0, row_count), "tp")


def local(
    tokens,
    segments,
    ln_gains,
    ln_biases,
    w_qkv,
    bias_qv,
    w_out,
    out_biases,
    w_up,
    up_bias,
    w_down,
    cotangent,
):
    gathered = (
        lax.all_gather(ln_gains, "fsdp", axis=1, tiled=True),
        lax.all_gather(ln_biases, "fsdp", axis=1, tiled=True),
        lax.all_gather(w_qkv, "fsdp", axis=1, tiled=True),
        lax.all_gather(bias_qv, "fsdp", axis=2, tiled=True),
        lax.all_gather(w_out, "fsdp", axis=1, tiled=True),
        lax.all_gather(out_biases, "fsdp", axis=1, tiled=True),
        lax.all_gather(w_up, "fsdp", axis=0, tiled=True),
        lax.all_gather(up_bias, "fsdp", axis=1, tiled=True),
        lax.all_gather(w_down, "fsdp", axis=1, tiled=True),
    )
    (
        gain_rows,
        shift_rows,
        qkv_proj,
        qv_bias,
        out_proj,
        branch_bias,
        up_proj,
        up_shift,
        down_proj,
    ) = gathered
    gain_rows = gain_rows.astype(jnp.float32)
    shift_rows = shift_rows.astype(jnp.float32)
    branch_bias = branch_bias.astype(jnp.float32)
    seq_count, block_len, width = tokens.shape
    row_count = seq_count * block_len
    width_heads = qkv_proj.shape[2]
    head_count = width_heads // HD
    inputs = tokens.astype(jnp.float32).reshape(row_count, width)
    cot_rows = cotangent.reshape(row_count, width)
    normed_low = layer_norm(inputs, gain_rows[0], shift_rows[0]).astype(jnp.bfloat16)
    projected = jnp.einsum("td,cdh->cth", normed_low, qkv_proj, preferred_element_type=jnp.float32)
    bias_flat = qv_bias.astype(jnp.float32).reshape(2, width_heads)
    query_low = (projected[0] + bias_flat[0]).astype(jnp.bfloat16)
    key_low = projected[1].astype(jnp.bfloat16)
    value_low = (projected[2] + bias_flat[1]).astype(jnp.bfloat16)
    pair_local = jnp.concatenate([key_low, value_low], axis=1).reshape(
        seq_count, block_len, 2 * width_heads
    )
    pair_rows, doc_rows = (
        lax.all_gather(pair_local, "ctx", axis=1, tiled=True),
        lax.all_gather(segments.astype(jnp.bfloat16), "ctx", axis=1, tiled=True),
    )
    full_len = pair_rows.shape[1]
    key_rows = pair_rows[:, :, :width_heads].reshape(seq_count, full_len, head_count, HD)
    value_rows = pair_rows[:, :, width_heads:].reshape(seq_count, full_len, head_count, HD)
    key_doc = doc_rows.astype(jnp.float32)
    key_place = jnp.arange(full_len, dtype=jnp.int32)
    block_rows = min(512, block_len)
    block_count = block_len // block_rows
    query_place = (
        lax.axis_index("ctx") * block_len + jnp.arange(block_len, dtype=jnp.int32)
    ).reshape(block_count, block_rows)
    query_doc = segments.astype(jnp.float32).reshape(seq_count, block_count, block_rows)
    query_blocks = query_low.reshape(seq_count, block_count, block_rows, head_count, HD)

    def forward_sequence(seq_item):
        seq_queries, seq_keys, seq_values, seq_key_doc, seq_query_doc = seq_item

        def forward_block(block_item):
            queries, places, doc_ids = block_item
            scores = block_scores(queries, seq_keys, places, doc_ids, key_place, seq_key_doc)
            row_max = jnp.max(scores, axis=-1, keepdims=True)
            exponent = jnp.exp(scores - row_max)
            totals = jnp.sum(exponent, axis=-1, keepdims=True)
            probability = (exponent / totals).astype(jnp.bfloat16)
            mixture = jnp.einsum(
                "hqk,khd->qhd", probability, seq_values, preferred_element_type=jnp.float32
            )
            return (mixture, (row_max + jnp.log(totals))[..., 0])

        return lax.map(forward_block, (seq_queries, query_place, seq_query_doc))

    mixture, log_sums = lax.map(
        forward_sequence, (query_blocks, key_rows, value_rows, key_doc, query_doc)
    )
    attended_low = mixture.reshape(row_count, width_heads).astype(jnp.bfloat16)

    def make_attn(start, count):
        return jnp.dot(attended_low, out_proj, preferred_element_type=jnp.float32)

    branch_part = tp_total(make_attn, row_count)
    hidden = inputs + branch_part + branch_bias[0]
    normed_two, norm_two_pull = jax.vjp(layer_norm, hidden, gain_rows[1], shift_rows[1])
    normed_two_own = normed_two.astype(jnp.bfloat16)
    pre_act = jnp.dot(
        normed_two_own, up_proj, preferred_element_type=jnp.float32
    ) + up_shift.astype(jnp.float32).reshape(-1)
    activated, gelu_pull = jax.vjp(gelu_tanh, pre_act)
    activated_low = activated.astype(jnp.bfloat16)

    def make_down(start, count):
        return jnp.dot(activated_low, down_proj, preferred_element_type=jnp.float32)

    second = tp_total(make_down, row_count) + branch_bias[1]
    result_own = (hidden + second).astype(jnp.bfloat16)
    qkv_back, out_back, up_back, down_back = (
        lax.all_gather(w_qkv, "fsdp", axis=1, tiled=True),
        lax.all_gather(w_out, "fsdp", axis=1, tiled=True),
        lax.all_gather(w_up, "fsdp", axis=0, tiled=True),
        lax.all_gather(w_down, "fsdp", axis=1, tiled=True),
    )
    grad_act_low = jnp.einsum(
        "td,fd->tf", cot_rows, down_back, preferred_element_type=jnp.float32
    ).astype(jnp.bfloat16)
    (grad_pre,) = gelu_pull(grad_act_low.astype(jnp.float32))
    grad_pre_low = grad_pre.astype(jnp.bfloat16)
    grad_down = jnp.einsum("tf,td->fd", activated_low, cot_rows, preferred_element_type=jnp.float32)
    grad_up = jnp.einsum(
        "td,tf->df", normed_two_own, grad_pre_low, preferred_element_type=jnp.float32
    )
    grad_up_bias = jnp.sum(grad_pre_low.astype(jnp.float32), axis=0).reshape(up_shift.shape)

    def make_mlp_back(start, count):
        return jnp.einsum("tf,df->td", grad_pre_low, up_back, preferred_element_type=jnp.float32)

    grad_normed_two = tp_total(make_mlp_back, row_count)
    grad_hidden_norm, grad_gain_two, grad_shift_two = norm_two_pull(grad_normed_two)
    grad_hidden = cot_rows.astype(jnp.float32) + grad_hidden_norm
    grad_branch_own = grad_hidden.astype(jnp.bfloat16)
    grad_out_proj = jnp.einsum(
        "th,td->hd", attended_low, grad_branch_own, preferred_element_type=jnp.float32
    )
    grad_attended = jnp.einsum(
        "td,hd->th", grad_branch_own, out_back, preferred_element_type=jnp.float32
    ).astype(jnp.bfloat16)
    grad_blocks = grad_attended.reshape(seq_count, block_count, block_rows, head_count, HD)

    def backward_sequence(seq_item):
        seq_queries, seq_grads, seq_logs, seq_keys, seq_values, seq_key_doc, seq_query_doc = (
            seq_item
        )

        def backward_block(running, block_item):
            key_sum, value_sum = running
            queries, grad_rows, log_sum, places, doc_ids = block_item
            scores = block_scores(queries, seq_keys, places, doc_ids, key_place, seq_key_doc)
            probability = jnp.exp(scores - log_sum[..., None])
            grad_prob = jnp.einsum(
                "qhd,khd->hqk", grad_rows, seq_values, preferred_element_type=jnp.float32
            )
            inner_sum = jnp.sum(probability * grad_prob, axis=-1, keepdims=True)
            grad_scores = (probability * (grad_prob - inner_sum) * 0.125).astype(jnp.bfloat16)
            grad_query = jnp.einsum(
                "hqk,khd->qhd", grad_scores, seq_keys, preferred_element_type=jnp.float32
            )
            key_sum = key_sum + jnp.einsum(
                "hqk,qhd->khd", grad_scores, queries, preferred_element_type=jnp.float32
            )
            value_sum = value_sum + jnp.einsum(
                "hqk,qhd->khd",
                probability.astype(jnp.bfloat16),
                grad_rows,
                preferred_element_type=jnp.float32,
            )
            return ((key_sum, value_sum), grad_query)

        zero_rows = jnp.zeros((full_len, head_count, HD), jnp.float32)
        (key_sum, value_sum), grad_query = lax.scan(
            backward_block,
            (zero_rows, zero_rows),
            (seq_queries, seq_grads, seq_logs, query_place, seq_query_doc),
        )
        return (key_sum, value_sum, grad_query)

    key_sum, value_sum, grad_query = lax.map(
        backward_sequence,
        (query_blocks, grad_blocks, log_sums, key_rows, value_rows, key_doc, query_doc),
    )
    pair_terms = jnp.concatenate(
        [
            key_sum.reshape(seq_count, full_len, width_heads),
            value_sum.reshape(seq_count, full_len, width_heads),
        ],
        axis=2,
    )
    pair_low = lax.psum_scatter(
        pair_terms.astype(jnp.bfloat16), "ctx", scatter_dimension=1, tiled=True
    ).reshape(row_count, 2 * width_heads)
    query_grad_low = grad_query.reshape(row_count, width_heads).astype(jnp.bfloat16)
    grad_proj_low = jnp.stack(
        [query_grad_low, pair_low[:, :width_heads], pair_low[:, width_heads:]]
    )
    grad_qkv = jnp.einsum(
        "td,cth->cdh", normed_low, grad_proj_low, preferred_element_type=jnp.float32
    )
    grad_qv_bias = jnp.stack(
        [
            jnp.sum(query_grad_low.astype(jnp.float32), axis=0),
            jnp.sum(pair_low[:, width_heads:].astype(jnp.float32), axis=0),
        ]
    ).reshape(qv_bias.shape)

    def make_qkv_back(start, count):
        return jnp.einsum(
            "cth,cdh->td", grad_proj_low, qkv_back, preferred_element_type=jnp.float32
        )

    grad_normed = tp_total(make_qkv_back, row_count)
    first_norm, first_pull = jax.vjp(layer_norm, inputs, gain_rows[0], shift_rows[0])
    grad_input_norm, grad_gain_one, grad_shift_one = first_pull(grad_normed)
    grad_tokens_own = grad_hidden + grad_input_norm
    norm_grads = jnp.stack([grad_gain_one, grad_gain_two, grad_shift_one, grad_shift_two])
    grad_gains = norm_grads[0:2]
    grad_shifts = norm_grads[2:4]
    grad_biases = jnp.stack(
        [
            jnp.sum(grad_branch_own.astype(jnp.float32), axis=0),
            jnp.sum(cot_rows.astype(jnp.float32), axis=0),
        ]
    )
    (
        part_gains,
        part_shifts,
        part_qkv,
        part_qv,
        part_out,
        part_biases,
        part_up,
        part_upb,
        part_down,
    ) = (
        lax.psum_scatter(
            grad_gains.astype(jnp.bfloat16), "fsdp", scatter_dimension=1, tiled=True
        ).astype(jnp.float32),
        lax.psum_scatter(
            grad_shifts.astype(jnp.bfloat16), "fsdp", scatter_dimension=1, tiled=True
        ).astype(jnp.float32),
        lax.psum_scatter(
            grad_qkv.astype(jnp.bfloat16), "fsdp", scatter_dimension=1, tiled=True
        ).astype(jnp.float32),
        lax.psum_scatter(
            grad_qv_bias.astype(jnp.bfloat16), "fsdp", scatter_dimension=2, tiled=True
        ).astype(jnp.float32),
        lax.psum_scatter(
            grad_out_proj.astype(jnp.bfloat16), "fsdp", scatter_dimension=1, tiled=True
        ).astype(jnp.float32),
        lax.psum_scatter(
            grad_biases.astype(jnp.bfloat16), "fsdp", scatter_dimension=1, tiled=True
        ).astype(jnp.float32),
        lax.psum_scatter(
            grad_up.astype(jnp.bfloat16), "fsdp", scatter_dimension=0, tiled=True
        ).astype(jnp.float32),
        lax.psum_scatter(
            grad_up_bias.astype(jnp.bfloat16), "fsdp", scatter_dimension=1, tiled=True
        ).astype(jnp.float32),
        lax.psum_scatter(
            grad_down.astype(jnp.bfloat16), "fsdp", scatter_dimension=1, tiled=True
        ).astype(jnp.float32),
    )
    reduced = (
        lax.psum(part_gains.astype(jnp.bfloat16), "ctx").astype(jnp.float32),
        lax.psum(part_shifts.astype(jnp.bfloat16), "ctx").astype(jnp.float32),
        lax.psum(part_qkv.astype(jnp.bfloat16), "ctx").astype(jnp.float32),
        lax.psum(part_qv.astype(jnp.bfloat16), "ctx").astype(jnp.float32),
        lax.psum(part_out.astype(jnp.bfloat16), "ctx").astype(jnp.float32),
        lax.psum(part_biases.astype(jnp.bfloat16), "ctx").astype(jnp.float32),
        lax.psum(part_up.astype(jnp.bfloat16), "ctx").astype(jnp.float32),
        lax.psum(part_upb.astype(jnp.bfloat16), "ctx").astype(jnp.float32),
        lax.psum(part_down.astype(jnp.bfloat16), "ctx").astype(jnp.float32),
    )
    result = result_own.reshape(seq_count, block_len, width)
    grad_tokens = grad_tokens_own.reshape(seq_count, block_len, width)
    return (
        result,
        grad_tokens,
        reduced[0],
        reduced[1],
        reduced[2],
        reduced[3],
        reduced[4],
        reduced[5],
        reduced[6],
        reduced[7],
        reduced[8],
    )


def solution(mesh):
    in_specs = (
        P("fsdp", "ctx", None),
        P("fsdp", "ctx"),
        P(None, "fsdp"),
        P(None, "fsdp"),
        P(None, "fsdp", "tp"),
        P(None, "tp", "fsdp"),
        P("tp", "fsdp"),
        P(None, "fsdp"),
        P("fsdp", "tp"),
        P("tp", "fsdp"),
        P("tp", "fsdp"),
        P("fsdp", "ctx", None),
    )
    out_specs = (
        P("fsdp", "ctx", None),
        P("fsdp", "ctx", None),
        P(None, "fsdp"),
        P(None, "fsdp"),
        P(None, "fsdp", "tp"),
        P(None, "tp", "fsdp"),
        P("tp", "fsdp"),
        P(None, "fsdp"),
        P("fsdp", "tp"),
        P("tp", "fsdp"),
        P("tp", "fsdp"),
    )
    return jax.shard_map(local, mesh=mesh, in_specs=in_specs, out_specs=out_specs, check_vma=False)
```

profile of v0, /device:TPU:0, one launch (start us, length us, event | category | flops | bytes accessed | tf_op | source)
XLA Modules:
  0.0 1358.0 jit_solution(1582386412131539376)
XLA Ops:
  26.1 13.1 all_gather.39
  65.3 16.4 %all-gather.7.cloned.1.call-done = bf16[2,1024,384]{1,0,2:T(2,128)(2,1)} async-done(((bf16[2,512,384]{1,0,2:T(2,128)(2,1)}), bf16[2,1024,384]{1,0,2:T(2,128)(2,1)}) %all-gather.7.cloned.1.call-update) | async-done | bytes 1572880 | tf_op jit(solution)/shard_map/all_gather | solution.py:91
  84.6 11.8 while.28
  112.6 107.9 %all-reduce.8.cloned.1.call-done = f32[1024,768]{1,0:T(8,128)} async-done(((f32[1024,768]{1,0:T(8,128)}), f32[1024,768]{1,0:T(8,128)}) %all-reduce.8.cloned.1.call-update) | async-done | bytes 3145744 | tf_op jit(solution)/shard_map/psum | solution.py:33
  243.0 119.9 %all-reduce.10.cloned.1.call-done = f32[1024,768]{1,0:T(8,128)} async-done(((f32[1024,768]{1,0:T(8,128)}), f32[1024,768]{1,0:T(8,128)}) %all-reduce.10.cloned.1.call-update) | async-done | bytes 3145744 | tf_op jit(solution)/shard_map/psum | solution.py:33
  372.2 73.2 %while.29 = (s32[]{:T(128)}, bf16[2,1024,3,64]{1,3,2,0:T(8,128)(2,1)}, bf16[2,1024,3,64]{1,3,2,0:T(8,128)(2,1)}, bf16[2,1,512,3,64]{2,4,3,1,0:T(8,128)(2,1)}, bf...) while((s32[]{:T(128)}, ...), condition=%wide.region_15.16_spmd.clone, body=%wide.region_13.15_spmd.clone.sunk | while | flops 1049105920 | bytes 106249448 | solution.py:216
  381.0 13.4 fusion.220
  394.4 14.2 %fusion.218 = bf16[2,1024,3,64]{1,3,2,0:T(8,128)(2,1)} fusion(bf16[2,1024,3,64]{1,3,2,0:T(8,128)(2,1)} %get-tuple-element.637, s32[]{:T(128)S(6)} %copy.159, f32[3,512,1024]{2,1,0:T(8,128)} %fusion.215, f32[3,512,1024]{2,1,0:T(8,128)} %copy-done, f32[3,512]{1,0:T(4,128)S(1)} %dynamic-slice_bitcast_fusion.2, pred[512,1024]{1,0:T(8,128)(4,1)S(1)} %fusion.217, ...), kind=kOutput, calls=%fused_computation.50.clone.1 | convolution fusion | flops 218630656 | bytes 27214848 | tf_op jit(solution)/shard_map/while/body/eval_jaxpr/while/body/eval_jaxpr/hqk,qhd->khd/dot_general | solution.py:197
  417.4 13.4 fusion.220
  430.8 14.2 %fusion.218 = bf16[2,1024,3,64]{1,3,2,0:T(8,128)(2,1)} fusion(bf16[2,1024,3,64]{1,3,2,0:T(8,128)(2,1)} %get-tuple-element.637, s32[]{:T(128)S(6)} %copy.159, f32[3,512,1024]{2,1,0:T(8,128)} %fusion.215, f32[3,512,1024]{2,1,0:T(8,128)} %copy-done, f32[3,512]{1,0:T(4,128)S(1)} %dynamic-slice_bitcast_fusion.2, pred[512,1024]{1,0:T(8,128)(4,1)S(1)} %fusion.217, ...), kind=kOutput, calls=%fused_computation.50.clone.1 | convolution fusion | flops 218630656 | bytes 27214848 | tf_op jit(solution)/shard_map/while/body/eval_jaxpr/while/body/eval_jaxpr/hqk,qhd->khd/dot_general | solution.py:197
  452.5 71.2 %copy.113 = bf16[2,1024,384]{0,2,1:T(8,128)(2,1)} copy(bf16[2,1024,384]{1,0,2:T(2,128)(2,1)} %pad_maximum_fusion) | data formatting | bytes 3145728
  523.7 162.7 %reshape.405 = bf16[1024,768]{1,0:T(8,128)(2,1)} reshape(bf16[1024,384,2]{2,1,0:T(8,128)(2,1)} %bitcast.53) | data formatting | bytes 3145728
  688.6 23.0 %reduce-scatter.31.cloned.1.call-done = bf16[512,768]{1,0:T(8,128)(2,1)} async-done(((bf16[1024,768]{1,0:T(8,128)(2,1)}), bf16[512,768]{1,0:T(8,128)(2,1)}) %reduce-scatter.31.cloned.1.call-update) | async-done | bytes 786448
  711.7 110.2 %reshape.406 = bf16[512,384,2]{2,1,0:T(8,128)(2,1)} reshape(bf16[512,768]{1,0:T(8,128)(2,1)} %reduce-scatter.31.cloned.1.call-done) | data formatting | bytes 1572864
  821.9 45.7 %copy.114 = bf16[2,512,384]{1,0,2:T(2,128)(2,1)S(1)} copy(bf16[2,512,384]{0,2,1:T(8,128)(2,1)} %bitcast.252) | data formatting | bytes 1572864
  902.9 26.1 %reduce-scatter.29.cloned.1.call-done = bf16[768,192]{0,1:T(8,128)(2,1)} async-done(((bf16[768,768]{0,1:T(8,128)(2,1)}), bf16[768,192]{0,1:T(8,128)(2,1)}) %reduce-scatter.29.cloned.1.call-update) | async-done | bytes 294928 | tf_op jit(solution)/shard_map/reduce_scatter | solution.py:297
  929.0 28.8 %reduce-scatter.27.cloned.1.call-done = bf16[192,768]{1,0:T(8,128)(2,1)} async-done(((bf16[768,768]{1,0:T(8,128)(2,1)}), bf16[192,768]{1,0:T(8,128)(2,1)}) %reduce-scatter.27.cloned.1.call-update) | async-done | bytes 294928 | tf_op jit(solution)/shard_map/reduce_scatter | solution.py:291
  967.5 12.2 reduce-scatter.45.cloned.1.call-done
  980.5 21.9 %reduce-scatter.43.cloned.1.call-done = bf16[192,2]{1,0:T(8,128)(2,1)} async-done(((bf16[768,2]{1,0:T(8,128)(2,1)}), bf16[192,2]{1,0:T(8,128)(2,1)}) %reduce-scatter.43.cloned.1.call-update) | async-done | bytes 784
  1003.3 21.1 %reduce-scatter.39.cloned.1.call-done = bf16[16,6]{1,0:T(8,128)(2,1)} async-done(((bf16[64,6]{1,0:T(8,128)(2,1)}), bf16[16,6]{1,0:T(8,128)(2,1)}) %reduce-scatter.39.cloned.1.call-update) | async-done | bytes 208
  1025.2 40.2 %all-reduce.14.cloned.1.call-done = (bf16[3,192,192]{1,2,0:T(8,128)(2,1)}, bf16[192,192]{1,0:T(8,128)(2,1)}, bf16[192,768]{1,0:T(8,128)(2,1)}, bf16[768,192]{0,1:T(8,128)(2,1)}) async-done(((bf16[3,192,192]{1,2,0:T(8,128)(2,1)}, bf16[192,192]{1,0:T(8,128)(2,1)}, bf16[192,768]{1,0:T(8,128)(2,1)}, bf16[768,192]{0,1:T(8,128)(2,1)}), (bf16[3,192,192]{1,2,0:T(8,128)(2,1)}, bf16[192,192]{1,0:T(8,128)(2,1)}, ...) | async-done | bytes 884752 | tf_op jit(solution)/shard_map/psum | solution.py:304
  1072.6 218.7 %all-reduce.12.cloned.1.call-done = (f32[1024,768]{1,0:T(8,128)}, f32[1024,768]{1,0:T(8,128)}) async-done(((f32[1024,768]{1,0:T(8,128)}, f32[1024,768]{1,0:T(8,128)}), (f32[1024,768]{1,0:T(8,128)}, f32[1024,768]{1,0:T(8,128)})) %all-reduce.12.cloned.1.call-update) | async-done | bytes 6291472 | tf_op jit(solution)/shard_map/psum | solution.py:33
  1304.9 14.4 %reduce-scatter.33.cloned.1.call-done = bf16[192,2]{1,0:T(8,128)(2,1)} async-done(((bf16[768,2]{1,0:T(8,128)(2,1)}), bf16[192,2]{1,0:T(8,128)(2,1)}) %reduce-scatter.33.cloned.1.call-update) | async-done | bytes 784
  1320.2 21.4 %reduce-scatter.35.cloned.1.call-done = bf16[192,2]{1,0:T(8,128)(2,1)} async-done(((bf16[768,2]{1,0:T(8,128)(2,1)}), bf16[192,2]{1,0:T(8,128)(2,1)}) %reduce-scatter.35.cloned.1.call-update) | async-done | bytes 784
  (343 shorter events, 210.6 us)
Async XLA Ops:
  8.0 73.6 %all-gather.7.cloned.1.call-start = ((), (), s32[]{:S(2)}) async-start(), calls=%async_computation.10 | async-start | bytes 2359296 | tf_op jit(solution)/shard_map/all_gather | solution.py:91
  53.0 167.5 %all-reduce.8.cloned.1.call-start = ((), (), s32[]{:S(2)}) async-start(), calls=%async_computation.11 | async-start | bytes 6291456 | tf_op jit(solution)/shard_map/psum | solution.py:33
  99.3 127.8 %all-gather.9.cloned.1.call-start = ((), (), s32[]{:S(2)}) async-start(), calls=%async_computation.12 | async-start | bytes 1474560 | tf_op jit(solution)/shard_map/all_gather | solution.py:57
  99.9 132.0 %all-gather.11.cloned.1.call-start = ((), (), s32[]{:S(2)}) async-start(), calls=%async_computation.13 | async-start | bytes 1474560 | tf_op jit(solution)/shard_map/all_gather | solution.py:59
  100.5 262.4 %all-reduce.10.cloned.1.call-start = ((), (), s32[]{:S(2)}) async-start(), calls=%async_computation.14 | async-start | bytes 6291456 | tf_op jit(solution)/shard_map/psum | solution.py:33
  242.6 469.0 %reduce-scatter.31.cloned.1.call-start = ((), (), s32[]{:S(2)}) async-start(), calls=%async_computation.17 | async-start | bytes 2359296
  523.7 162.8 %copy-start.22 = (bf16[24,8,2,512]{3,1,2,0:T(8,128)(2,1)S(1)}, bf16[24,8,2,512]{3,1,2,0:T(8,128)(2,1)}, u32[]{:S(2)}) copy-start(bf16[24,8,2,512]{3,1,2,0:T(8,128)(2,1)} %copy-done.21) | copy-start | bytes 1179652
  686.4 202.1 %reduce-scatter.41.cloned.1.call-start = ((), (), s32[]{:S(2)}) async-start(), calls=%async_computation.22 | async-start | bytes 491520
  687.9 212.9 %reduce-scatter.37.cloned.1.call-start = ((), (), s32[]{:S(2)}) async-start(), calls=%async_computation.20 | async-start | bytes 1228800
  688.6 179.2 %copy-start.28 = (bf16[1,1024,192]{1,2,0:T(8,128)(2,1)}, bf16[1,1024,192]{1,2,0:T(8,128)(2,1)S(1)}, u32[]{:S(2)}) copy-start(bf16[1,1024,192]{1,2,0:T(8,128)(2,1)S(1)} %convert_element_type.214) | copy-start | bytes 1179652
  876.2 52.8 %reduce-scatter.29.cloned.1.call-start = ((), (), s32[]{:S(2)}) async-start(), calls=%async_computation.16 | async-start | bytes 1474560 | tf_op jit(solution)/shard_map/reduce_scatter | solution.py:297
  881.1 76.6 %reduce-scatter.27.cloned.1.call-start = ((), (), s32[]{:S(2)}) async-start(), calls=%async_computation.15 | async-start | bytes 1474560 | tf_op jit(solution)/shard_map/reduce_scatter | solution.py:291
  885.1 94.6 %reduce-scatter.45.cloned.1.call-start = ((), (), s32[]{:S(2)}) async-start(), calls=%async_computation.24 | async-start | bytes 20480
  886.3 116.1 %reduce-scatter.43.cloned.1.call-start = ((), (), s32[]{:S(2)}) async-start(), calls=%async_computation.23 | async-start | bytes 245760
  887.4 137.0 %reduce-scatter.39.cloned.1.call-start = ((), (), s32[]{:S(2)}) async-start(), calls=%async_computation.21 | async-start | bytes 20480
  888.4 177.1 %all-reduce.14.cloned.1.call-start = ((), (), s32[]{:S(2)}) async-start(), calls=%async_computation.26 | async-start | bytes 1966080 | tf_op jit(solution)/shard_map/psum | solution.py:304
  957.8 333.5 %all-reduce.12.cloned.1.call-start = ((), (), s32[]{:S(2)}) async-start(), calls=%async_computation.25 | async-start | bytes 12582912 | tf_op jit(solution)/shard_map/psum | solution.py:33
  967.4 324.0 %copy-start.4 = (bf16[2,512,768]{2,1,0:T(8,128)(2,1)S(1)}, bf16[2,512,768]{2,1,0:T(8,128)(2,1)}, u32[]{:S(2)}) copy-start(bf16[2,512,768]{2,1,0:T(8,128)(2,1)} %param.16) | copy-start | bytes 4718596
  967.4 324.0 %copy-start.36 = (f32[768]{0:T(1024)S(1)}, f32[768]{0:T(1024)}, u32[]{:S(2)}) copy-start(f32[768]{0:T(1024)} %copy-done.35) | copy-start | bytes 9220
  967.4 324.0 %copy-start.38 = (f32[1,4,2,128]{3,1,2,0:T(4,128)S(1)}, f32[1,4,2,128]{3,1,2,0:T(4,128)}, u32[]{:S(2)}) copy-start(f32[1,4,2,128]{3,1,2,0:T(4,128)} %copy-done.37) | copy-start | bytes 12292
  967.4 351.9 %reduce-scatter.33.cloned.1.call-start = ((), (), s32[]{:S(2)}) async-start(), calls=%async_computation.18 | async-start | bytes 245760
  1069.0 225.4 %copy-start.52 = (f32[1,4,2,128]{3,1,2,0:T(4,128)S(1)}, f32[1,4,2,128]{3,1,2,0:T(4,128)}, u32[]{:S(2)}) copy-start(f32[1,4,2,128]{3,1,2,0:T(4,128)} %copy-done.51) | copy-start | bytes 12292
  1069.0 225.4 %copy-start.42 = (f32[1024]{0:T(1024)S(1)}, f32[1024]{0:T(1024)}, u32[]{:S(2)}) copy-start(f32[1024]{0:T(1024)} %copy-done.41) | copy-start | bytes 12292
  1300.5 41.1 %reduce-scatter.35.cloned.1.call-start = ((), (), s32[]{:S(2)}) async-start(), calls=%async_computation.19 | async-start | bytes 245760
  (62 other events, 478.5 us)
Sparse Core Ops, SparseCore 0:
  53.1 28.4 all-gather.6
  99.4 121.0 all-reduce.7
  242.8 120.0 all-reduce.9
  686.5 25.1 reduce-scatter.30
  714.0 20.8 reduce-scatter.40
  876.3 24.4 reduce-scatter.36
  903.4 25.5 reduce-scatter.28
  932.1 25.6 reduce-scatter.26
  960.2 19.4 reduce-scatter.44
  982.6 19.7 reduce-scatter.42
  1004.8 19.4 reduce-scatter.38
  1026.7 38.6 all-reduce.13
  1068.4 222.8 all-reduce.11
Sparse Core Ops, SparseCore 1:
  101.3 17.3 all-gather.8
  120.1 17.2 all-gather.10
  1300.5 18.7 reduce-scatter.32
  1321.7 19.8 reduce-scatter.34
where the time goes:
time: 1370 us; the launch traced here: 1360 us
  waiting for transfers between devices  684 us (50%)
  local copies, waits for them, and re-layouts  436 us (32%)
  matrix products  116 us (8%)
  blocking collectives  56.8 us (4%)
  other arithmetic  46.8 us (3%)
  between operations  16.9 us (1%)
    psum x3, waiting for transfers between devices, tp_total(): return lax.psum(make(0, row_count), 'tp')  447 us
    unnamed x159, local copies, waits for them, and re-layouts  418 us
    unnamed x25, waiting for transfers between devices  126 us
    psum x1, waiting for transfers between devices, local(): lax.psum(part_qkv.astype(jnp.bfloat16), 'ctx').astype(jnp.float32)  40.2 us
    reduce_scatter x1, waiting for transfers between devices, local(): lax.psum_scatter(grad_up.astype(jnp.bfloat16), 'fsdp', scatter_dimension=...  28.8 us
    dot_general x2, matrix products, backward_block(): jnp.einsum('hqk,qhd->khd', grad_scores, queries, preferred_element_type=j...  28.4 us
  transfers between devices with their start and end apart: 17, of which 14 were waited for; matrix products, arithmetic and copies ran while one was open for 16% of the time, Pallas kernels for 0%

commit v1 on v0

--- a/solution.py
+++ b/solution.py
@@ -301,7 +301,7 @@
     reduced = (
         lax.psum(part_gains.astype(jnp.bfloat16), "ctx").astype(jnp.float32),
         lax.psum(part_shifts.astype(jnp.bfloat16), "ctx").astype(jnp.float32),
-        lax.psum(part_qkv.astype(jnp.bfloat16), "ctx").astype(jnp.float32),
+        jnp.sum(lax.all_gather(part_qkv.astype(jnp.bfloat16), "ctx"), axis=0).astype(jnp.float32),
         lax.psum(part_qv.astype(jnp.bfloat16), "ctx").astype(jnp.float32),
         lax.psum(part_out.astype(jnp.bfloat16), "ctx").astype(jnp.float32),
         lax.psum(part_biases.astype(jnp.bfloat16), "ctx").astype(jnp.float32),

time: 1370 us -> 1190 us (0.87)
  waiting for transfers between devices: 684 us -> 504 us
    unnamed x25, waiting for transfers between devices: 126 us -> 81 us
    psum x1, waiting for transfers between devices: 40.2 us -> 0.01 us  [local(): lax.psum(part_out.astype(jnp.bfloat16), 'ctx').astype(jnp.float32)]
    psum x3, waiting for transfers between devices: 447 us -> 407 us  [tp_total(): return lax.psum(make(0, row_count), 'tp')]
    reduce_scatter x1, waiting for transfers between devices: 28.8 us -> 0.01 us  [local(): lax.psum_scatter(grad_up.astype(jnp.bfloat16), 'fsdp', scatter_dimension=...]
    reduce_scatter x1, waiting for transfers between devices: 26.1 us -> 0.01 us  [local(): lax.psum_scatter(grad_down.astype(jnp.bfloat16), 'fsdp', scatter_dimensio...]
    unnamed x159 -> x155, local copies, waits for them, and re-layouts: 418 us -> 414 us
  transfers between devices with their start and end apart: 17 -> 17, of which waited for: 14 -> 8; matrix products, arithmetic and copies ran while one was open for 16% -> 45% of each run, Pallas kernels for 0% -> 0%
where the time goes in v1:
time: 1190 us
  waiting for transfers between devices  504 us (42%)
  local copies, waits for them, and re-layouts  437 us (37%)
  matrix products  116 us (10%)
  blocking collectives  66.2 us (6%)
  other arithmetic  45.1 us (4%)
  between operations  16.9 us (1%)
    unnamed x155, local copies, waits for them, and re-layouts  414 us
    psum x3, waiting for transfers between devices, tp_total(): return lax.psum(make(0, row_count), 'tp')  407 us
    unnamed x25, waiting for transfers between devices  81 us
    dot_general x2, matrix products, backward_block(): jnp.einsum('hqk,qhd->khd', grad_scores, queries, preferred_element_type=j...  28.7 us
    dot_general x2, matrix products, backward_block(): jnp.einsum('hqk,khd->qhd', grad_scores, seq_keys, preferred_element_type=...  25.5 us
  transfers between devices with their start and end apart: 17, of which 8 were waited for; matrix products, arithmetic and copies ran while one was open for 45% of the time, Pallas kernels for 0%

profile of v1, /device:TPU:0, one launch (start us, length us, event | category | flops | bytes accessed | tf_op | source)
XLA Modules:
  0.0 1186.5 jit_solution(1981374954915849868)
XLA Ops:
  8.1 6.4 all-gather.1
  26.1 13.1 %all_gather.45 = bf16[3,768,192]{2,0,1:T(4,128)(2,1)S(1)} all-gather(bf16[3,192,192]{2,0,1:T(4,128)(2,1)S(1)} %copy.95), channel_id=1, replica_groups=mesh['fsdp'=4,'ctx'=2,'tp'=4] {'fsdp'}, dimensions={1}, use_global_device_ids=true | all-gather | bytes 1105920 | tf_op jit(solution)/shard_map/all_gather | solution.py:53
  58.3 6.8 all_gather.49
  65.3 16.3 %all-gather.8.cloned.1.call-done = bf16[2,1024,384]{1,0,2:T(2,128)(2,1)} async-done(((bf16[2,512,384]{1,0,2:T(2,128)(2,1)}), bf16[2,1024,384]{1,0,2:T(2,128)(2,1)}) %all-gather.8.cloned.1.call-update) | async-done | bytes 1572880 | tf_op jit(solution)/shard_map/all_gather | solution.py:91
  84.6 11.8 while.28
  112.8 107.7 %all-reduce.8.cloned.1.call-done = f32[1024,768]{1,0:T(8,128)} async-done(((f32[1024,768]{1,0:T(8,128)}), f32[1024,768]{1,0:T(8,128)}) %all-reduce.8.cloned.1.call-update) | async-done | bytes 3145744 | tf_op jit(solution)/shard_map/psum | solution.py:33
  231.9 6.4 fusion.155
  242.6 120.2 %all-reduce.10.cloned.1.call-done = f32[1024,768]{1,0:T(8,128)} async-done(((f32[1024,768]{1,0:T(8,128)}), f32[1024,768]{1,0:T(8,128)}) %all-reduce.10.cloned.1.call-update) | async-done | bytes 3145744 | tf_op jit(solution)/shard_map/psum | solution.py:33
  385.1 73.9 %while.29 = (s32[]{:T(128)}, bf16[2,1024,3,64]{1,3,2,0:T(8,128)(2,1)}, bf16[2,1024,3,64]{1,3,2,0:T(8,128)(2,1)}, bf16[2,1,512,3,64]{2,4,3,1,0:T(8,128)(2,1)S(1)}...) while((s32[]{:T(128)}, ...), condition=%wide.region_15.16_spmd.clone, body=%wide.region_13.15_spmd.clone.sunk | while | flops 1049105920 | bytes 107822312 | solution.py:216
  394.8 12.9 %fusion.220 = bf16[2,1,512,3,64]{2,4,3,1,0:T(8,128)(2,1)S(1)} fusion(bf16[2,1,512,3,64]{2,4,3,1,0:T(8,128)(2,1)S(1)} %get-tuple-element.627, s32[]{:T(128)S(6)} %copy.165, f32[3,512,1024]{2,1,0:T(8,128)} %fusion.215, f32[3,512,1024]{2,1,0:T(8,128)} %copy-done, f32[3,512]{1,0:T(4,128)S(1)} %dynamic-slice_bitcast_fusion.2, ...), kind=kOutput, calls=%fused_computation.54.clone.1 | convolution fusion | flops 218630656 | bytes 27018240 | tf_op jit(solution)/shard_map/while/body/eval_jaxpr/while/body/eval_jaxpr/hqk,khd->qhd/dot_general | solution.py:194
  407.7 14.4 %fusion.218 = bf16[2,1024,3,64]{1,3,2,0:T(8,128)(2,1)} fusion(bf16[2,1024,3,64]{1,3,2,0:T(8,128)(2,1)} %get-tuple-element.625, s32[]{:T(128)S(6)} %copy.165, f32[3,512,1024]{2,1,0:T(8,128)} %fusion.215, f32[3,512,1024]{2,1,0:T(8,128)} %copy-done, f32[3,512]{1,0:T(4,128)S(1)} %dynamic-slice_bitcast_fusion.2, pred[512,1024]{1,0:T(8,128)(4,1)S(1)} %fusion.217, ...), kind=kOutput, calls=%fused_computation.50.clone.1 | convolution fusion | flops 218630656 | bytes 27214848 | tf_op jit(solution)/shard_map/while/body/eval_jaxpr/while/body/eval_jaxpr/hqk,qhd->khd/dot_general | solution.py:197
  431.8 12.7 %fusion.220 = bf16[2,1,512,3,64]{2,4,3,1,0:T(8,128)(2,1)S(1)} fusion(bf16[2,1,512,3,64]{2,4,3,1,0:T(8,128)(2,1)S(1)} %get-tuple-element.627, s32[]{:T(128)S(6)} %copy.165, f32[3,512,1024]{2,1,0:T(8,128)} %fusion.215, f32[3,512,1024]{2,1,0:T(8,128)} %copy-done, f32[3,512]{1,0:T(4,128)S(1)} %dynamic-slice_bitcast_fusion.2, ...), kind=kOutput, calls=%fused_computation.54.clone.1 | convolution fusion | flops 218630656 | bytes 27018240 | tf_op jit(solution)/shard_map/while/body/eval_jaxpr/while/body/eval_jaxpr/hqk,khd->qhd/dot_general | solution.py:194
  444.5 14.3 %fusion.218 = bf16[2,1024,3,64]{1,3,2,0:T(8,128)(2,1)} fusion(bf16[2,1024,3,64]{1,3,2,0:T(8,128)(2,1)} %get-tuple-element.625, s32[]{:T(128)S(6)} %copy.165, f32[3,512,1024]{2,1,0:T(8,128)} %fusion.215, f32[3,512,1024]{2,1,0:T(8,128)} %copy-done, f32[3,512]{1,0:T(4,128)S(1)} %dynamic-slice_bitcast_fusion.2, pred[512,1024]{1,0:T(8,128)(4,1)S(1)} %fusion.217, ...), kind=kOutput, calls=%fused_computation.50.clone.1 | convolution fusion | flops 218630656 | bytes 27214848 | tf_op jit(solution)/shard_map/while/body/eval_jaxpr/while/body/eval_jaxpr/hqk,qhd->khd/dot_general | solution.py:197
  464.9 71.7 %copy.117 = bf16[2,1024,384]{0,2,1:T(8,128)(2,1)} copy(bf16[2,1024,384]{1,0,2:T(2,128)(2,1)S(1)} %pad_maximum_fusion) | data formatting | bytes 3145728
  536.6 162.8 %reshape.406 = bf16[1024,768]{1,0:T(8,128)(2,1)} reshape(bf16[1024,384,2]{2,1,0:T(8,128)(2,1)} %bitcast.54) | data formatting | bytes 3145728
  705.2 19.7 %reduce-scatter.31.cloned.1.call-done = bf16[512,768]{1,0:T(8,128)(2,1)} async-done(((bf16[1024,768]{1,0:T(8,128)(2,1)}), bf16[512,768]{1,0:T(8,128)(2,1)}) %reduce-scatter.31.cloned.1.call-update) | async-done | bytes 786448
  725.0 110.0 %reshape.407 = bf16[512,384,2]{2,1,0:T(8,128)(2,1)} reshape(bf16[512,768]{1,0:T(8,128)(2,1)} %reduce-scatter.31.cloned.1.call-done) | data formatting | bytes 1572864
  835.0 45.7 %copy.118 = bf16[2,512,384]{1,0,2:T(2,128)(2,1)S(1)} copy(bf16[2,512,384]{0,2,1:T(8,128)(2,1)} %bitcast.253) | data formatting | bytes 1572864
  887.8 5.9 fusion.144
  904.9 24.1 %reduce-scatter.37.cloned.1.call-done = bf16[192,576]{1,0:T(8,128)(2,1)} async-done(((bf16[768,576]{1,0:T(8,128)(2,1)}), bf16[192,576]{1,0:T(8,128)(2,1)}) %reduce-scatter.37.cloned.1.call-update) | async-done | bytes 221200
  930.2 9.2 all-gather
  940.8 179.1 %all-reduce.12.cloned.1.call-done = (f32[1024,768]{1,0:T(8,128)}, f32[1024,768]{1,0:T(8,128)}) async-done(((f32[1024,768]{1,0:T(8,128)}, f32[1024,768]{1,0:T(8,128)}), (f32[1024,768]{1,0:T(8,128)}, f32[1024,768]{1,0:T(8,128)})) %all-reduce.12.cloned.1.call-update) | async-done | bytes 6291472 | tf_op jit(solution)/shard_map/psum | solution.py:33
  1133.4 14.4 %reduce-scatter.33.cloned.1.call-done = bf16[192,2]{1,0:T(8,128)(2,1)} async-done(((bf16[768,2]{1,0:T(8,128)(2,1)}), bf16[192,2]{1,0:T(8,128)(2,1)}) %reduce-scatter.33.cloned.1.call-update) | async-done | bytes 784
  1148.7 21.4 %reduce-scatter.35.cloned.1.call-done = bf16[192,2]{1,0:T(8,128)(2,1)} async-done(((bf16[768,2]{1,0:T(8,128)(2,1)}), bf16[192,2]{1,0:T(8,128)(2,1)}) %reduce-scatter.35.cloned.1.call-update) | async-done | bytes 784
  (342 shorter events, 174.2 us)
Async XLA Ops:
  8.0 73.6 %all-gather.8.cloned.1.call-start = ((), (), s32[]{:S(2)}) async-start(), calls=%async_computation.10 | async-start | bytes 2359296 | tf_op jit(solution)/shard_map/all_gather | solution.py:91
  53.0 167.5 %all-reduce.8.cloned.1.call-start = ((), (), s32[]{:S(2)}) async-start(), calls=%async_computation.11 | async-start | bytes 6291456 | tf_op jit(solution)/shard_map/psum | solution.py:33
  99.3 127.8 %all-gather.10.cloned.1.call-start = ((), (), s32[]{:S(2)}) async-start(), calls=%async_computation.12 | async-start | bytes 1474560 | tf_op jit(solution)/shard_map/all_gather | solution.py:57
  99.9 132.0 %all-gather.12.cloned.1.call-start = ((), (), s32[]{:S(2)}) async-start(), calls=%async_computation.13 | async-start | bytes 1474560 | tf_op jit(solution)/shard_map/all_gather | solution.py:59
  100.5 262.3 %all-reduce.10.cloned.1.call-start = ((), (), s32[]{:S(2)}) async-start(), calls=%async_computation.14 | async-start | bytes 6291456 | tf_op jit(solution)/shard_map/psum | solution.py:33
  223.3 143.2 %copy-start.1 = (f32[1024,768]{1,0:T(8,128)}, f32[1024,768]{1,0:T(8,128)S(1)}, u32[]{:S(2)}) copy-start(f32[1024,768]{1,0:T(8,128)S(1)} %get-tuple-element.431) | copy-start | bytes 9437188
  242.6 459.3 %reduce-scatter.41.cloned.1.call-start = ((), (), s32[]{:S(2)}) async-start(), calls=%async_computation.22 | async-start | bytes 491520
  371.1 332.5 %reduce-scatter.29.cloned.1.call-start = ((), (), s32[]{:S(2)}) async-start(), calls=%async_computation.16 | async-start | bytes 1474560 | tf_op jit(solution)/shard_map/reduce_scatter | solution.py:297
  376.4 327.2 %reduce-scatter.27.cloned.1.call-start = ((), (), s32[]{:S(2)}) async-start(), calls=%async_computation.15 | async-start | bytes 1474560 | tf_op jit(solution)/shard_map/reduce_scatter | solution.py:291
  381.1 343.8 %reduce-scatter.31.cloned.1.call-start = ((), (), s32[]{:S(2)}) async-start(), calls=%async_computation.17 | async-start | bytes 2359296
  536.6 162.9 %copy-start.12 = (bf16[2,512,768]{2,1,0:T(8,128)(2,1)S(1)}, bf16[2,512,768]{2,1,0:T(8,128)(2,1)}, u32[]{:S(2)}) copy-start(bf16[2,512,768]{2,1,0:T(8,128)(2,1)} %param.27) | copy-start | bytes 4718596
  699.4 197.5 %reduce-scatter.45.cloned.1.call-start = ((), (), s32[]{:S(2)}) async-start(), calls=%async_computation.24 | async-start | bytes 20480
  700.9 196.9 %reduce-scatter.43.cloned.1.call-start = ((), (), s32[]{:S(2)}) async-start(), calls=%async_computation.23 | async-start | bytes 245760
  701.8 196.8 %all-reduce.14.cloned.1.call-start = ((), (), s32[]{:S(2)}) async-start(), calls=%async_computation.26 | async-start | bytes 1376256 | tf_op jit(solution)/shard_map/psum | solution.py:306
  703.6 200.5 %reduce-scatter.39.cloned.1.call-start = ((), (), s32[]{:S(2)}) async-start(), calls=%async_computation.21 | async-start | bytes 20480
  881.9 47.1 %reduce-scatter.37.cloned.1.call-start = ((), (), s32[]{:S(2)}) async-start(), calls=%async_computation.20 | async-start | bytes 1228800
  887.8 232.1 %all-reduce.12.cloned.1.call-start = ((), (), s32[]{:S(2)}) async-start(), calls=%async_computation.25 | async-start | bytes 12582912 | tf_op jit(solution)/shard_map/psum | solution.py:33
  896.8 250.9 %reduce-scatter.33.cloned.1.call-start = ((), (), s32[]{:S(2)}) async-start(), calls=%async_computation.18 | async-start | bytes 245760
  900.2 219.6 %copy-start.4 = (bf16[2,512,768]{2,1,0:T(8,128)(2,1)S(1)}, bf16[2,512,768]{2,1,0:T(8,128)(2,1)}, u32[]{:S(2)}) copy-start(bf16[2,512,768]{2,1,0:T(8,128)(2,1)} %param.16) | copy-start | bytes 4718596
  900.2 219.6 %copy-start.33 = (f32[768]{0:T(1024)S(1)}, f32[768]{0:T(1024)}, u32[]{:S(2)}) copy-start(f32[768]{0:T(1024)} %copy-done.32) | copy-start | bytes 9220
  900.2 219.7 %copy-start.35 = (f32[1,4,2,128]{3,1,2,0:T(4,128)S(1)}, f32[1,4,2,128]{3,1,2,0:T(4,128)}, u32[]{:S(2)}) copy-start(f32[1,4,2,128]{3,1,2,0:T(4,128)} %copy-done.34) | copy-start | bytes 12292
  939.6 183.2 %copy-start.49 = (f32[1,4,2,128]{3,1,2,0:T(4,128)S(1)}, f32[1,4,2,128]{3,1,2,0:T(4,128)}, u32[]{:S(2)}) copy-start(f32[1,4,2,128]{3,1,2,0:T(4,128)} %copy-done.48) | copy-start | bytes 12292
  939.6 183.2 %copy-start.39 = (f32[1024]{0:T(1024)S(1)}, f32[1024]{0:T(1024)}, u32[]{:S(2)}) copy-start(f32[1024]{0:T(1024)} %copy-done.38) | copy-start | bytes 12292
  1129.0 41.1 %reduce-scatter.35.cloned.1.call-start = ((), (), s32[]{:S(2)}) async-start(), calls=%async_computation.19 | async-start | bytes 245760
  (60 other events, 292.9 us)
Sparse Core Ops, SparseCore 0:
  53.1 28.4 all-gather.7
  99.4 121.0 all-reduce.7
  242.7 120.0 all-reduce.9
  704.8 43.3 all-reduce.13
  897.0 222.8 all-reduce.11
Sparse Core Ops, SparseCore 1:
  101.4 17.3 all-gather.9
  120.2 17.2 all-gather.11
  371.2 19.7 reduce-scatter.40
  393.6 25.6 reduce-scatter.28
  421.8 25.5 reduce-scatter.26
  699.5 25.4 reduce-scatter.30
  727.2 19.5 reduce-scatter.44
  749.6 19.7 reduce-scatter.42
  882.0 19.5 reduce-scatter.38
  904.7 24.3 reduce-scatter.36
  1129.0 18.7 reduce-scatter.32
  1150.3 19.8 reduce-scatter.34
